TPU v7x, 128 devices: a whole 4x4x4 slice. The times are simulated.
128 devices in a mesh: cols: 128 (over x, z, y, core).
Axes of the slice: x: 4, y: 4, z: 4, core: 2. Of those that a mesh axis runs over, the one named last changes fastest.
Arguments:
- suction_initial: float32 [128, 65536], P(None, 'cols'), may hold values from -6 to 6
- warmth_initial: float32 [128, 65536], P(None, 'cols'), may hold values from -5 to 5
- soil_class: int32 [128, 65536], P(None, 'cols'), may hold values from 0 to 7
- top_boundary_warmth: float32 [65536], P('cols'), may hold values from -6 to 6
- neighbour_couplings: int32 [2, 512], replicated, may hold values from 0 to 1
- k_sat: float32 [8], replicated, may hold values from 0.1 to 1
- heat_cond: float32 [8], replicated, may hold values from 0.5 to 2
Outputs:
- suction_iterated: float32 [128, 65536], P(None, 'cols')
- warmth_iterated: float32 [128, 65536], P(None, 'cols')
All inputs are finite; a program needn't handle non-finite values.
Results may differ from a plain program's by a relative error of at most 0.000066.
Values sent between devices are 32-bit elements; how exact they have to be, the bound alone decides.
A program may use at most 128 MiB of HBM per device.

v0:
```python
import functools

import jax
import jax.numpy as jnp
from jax import lax
from jax.experimental import pallas as pl
from jax.experimental.pallas import tpu as pltpu
from jax.sharding import PartitionSpec as P

MESH = pl.DeviceIdType.MESH

SPAN = 256
LANES = 128
HALVES = SPAN // LANES
BLOCKS = 2
ROWS = 128
CHUNK = 16
PAIR_DEV = 4

W, P1, M1, P1X, M1X, P2, M2, X2 = range(8)
SLOTS = 8
MESSAGES = 10


def sig(v):
    return 1.0 / (1.0 + jnp.exp(-v))


def message(step, half, field):
    return half * 3 + field if step == 0 else 6 + half * 2 + field


def lookup(table, classes):
    result = jnp.full(classes.shape, table[0], jnp.float32)
    for entry in range(1, table.shape[0]):
        result = jnp.where(classes == entry, table[entry], result)
    return result


def down(value):
    return pltpu.roll(value, 1, 1)


def up(value):
    return pltpu.roll(value, 7, 1)


def strided(row):
    return pl.ds(row, 8, stride=CHUNK)


def forward_row(row, coef, main, above, below, source, carry):
    c_ref, a_ref, d_ref = coef
    c_prev, a_prev, d_prev = carry
    inverse = 1.0 / (main + above * c_prev)
    c_new = -below * inverse
    a_new = above * a_prev * inverse
    d_new = (source + above * d_prev) * inverse
    c_ref[row] = c_new
    a_ref[row] = a_new
    d_ref[row] = d_new
    return c_new, a_new, d_new


def finish(coef, last, write):
    c_ref, a_ref, d_ref = coef
    c_last, a_last, d_last = last
    zero = jnp.zeros_like(c_last)

    def gather(step, carry):
        d_sum, a_sum, g_sum = carry
        row = CHUNK - 2 - step
        c_row = c_ref[row]
        return d_ref[row] - c_row * d_sum, a_ref[row] - c_row * a_sum, -c_row * g_sum

    d_sum, a_sum, g_sum = lax.fori_loop(0, CHUNK - 1, gather, (zero, zero, zero - 1.0), unroll=True)
    inverse = 1.0 / (1.0 - c_last * up(a_sum))
    alpha = a_last * inverse
    gamma = -c_last * up(g_sum) * inverse
    delta = (d_last - c_last * up(d_sum)) * inverse
    for shift in (1, 2, 4):
        back = functools.partial(pltpu.roll, shift=shift, axis=1)
        ahead = functools.partial(pltpu.roll, shift=8 - shift, axis=1)
        inverse = 1.0 / (1.0 - alpha * back(gamma) - gamma * ahead(alpha))
        delta = (delta - alpha * back(delta) - gamma * ahead(delta)) * inverse
        if shift < 4:
            alpha, gamma = -alpha * back(alpha) * inverse, -gamma * ahead(gamma) * inverse
    before = down(delta)
    write(CHUNK - 1, delta)

    def back_row(step, later):
        row = CHUNK - 2 - step
        value = (d_ref[row] - a_ref[row] * before) - c_ref[row] * later
        write(row, value)
        return value

    lax.fori_loop(0, CHUNK - 1, back_row, delta, unroll=True)


def kernel(
    devices,
    head_hbm,
    warmth_hbm,
    class_hbm,
    top_ref,
    couplings,
    k_table,
    lam_table,
    head_out,
    warmth_out,
    own,
    rx,
    result,
    classes,
    lam,
    sat,
    melt,
    cond,
    energy_old,
    lat_water,
    lat_heat,
    c_ref,
    a_ref,
    d_ref,
    load_sem,
    store_sem,
    send_sem,
    recv_sem,
):
    me = lax.axis_index("cols")
    core = lax.rem(me, 2)
    other = me + 1 - 2 * core
    ahead = lax.rem(me + 2, devices)
    behind = lax.rem(me + devices - 2, devices)
    coef = (c_ref, a_ref, d_ref)

    def columns(half, block):
        return pl.ds(block * SPAN + half * LANES, LANES)

    def load(half, field, block):
        source = (head_hbm, warmth_hbm, class_hbm)[field]
        target = classes.at[half, block] if field == 2 else own.at[message(0, half, field), block]
        return pltpu.make_async_copy(
            source.at[:, columns(half, block)], target, load_sem.at[half, field, block]
        )

    def store(half, field, block):
        target = (head_out, warmth_out)[field]
        return pltpu.make_async_copy(
            result.at[half, field, block],
            target.at[:, columns(half, block)],
            store_sem.at[half, field, block],
        )

    def copy(slot, index):
        if slot in (W, P1, M1):
            source = own.at[index]
        elif slot in (P1X, P2):
            source = rx.at[P1, index]
        elif slot in (M1X, M2):
            source = rx.at[M1, index]
        else:
            source = rx.at[M2 - core * (M2 - P2), index]
        target = {P1: ahead, P2: ahead, M1: behind, M2: behind}.get(slot, other)
        return pltpu.make_async_remote_copy(
            src_ref=source,
            dst_ref=rx.at[slot, index],
            send_sem=send_sem.at[slot, index],
            recv_sem=recv_sem.at[slot, index],
            device_id=(target,),
            device_id_type=MESH,
        )

    def lookups(half):
        def body(tile, carry):
            rows = pl.ds(pl.multiple_of(tile * 8, 8), 8)
            for block in range(BLOCKS):
                kinds = classes[half, block, rows, :]
                own[message(0, half, 2), block, rows, :] = lookup(k_table, kinds)
                lam[half, block, rows, :] = lookup(lam_table, kinds)
            return carry

        lax.fori_loop(0, ROWS // 8, body, 0)

    def prepare(step, half):
        def body(tile, carry):
            rows = pl.ds(pl.multiple_of(tile * 8, 8), 8)
            for block in range(BLOCKS):
                head = own[message(step, half, 0), block, rows, :]
                warmth = own[message(step, half, 1), block, rows, :]
                filled = sig(head)
                liquid = sig(2.0 * warmth)
                sat[step, half, block, rows, :] = filled
                melt[half, block, rows, :] = liquid
                cond[half, block, rows, :] = own[message(0, half, 2), block, rows, :] * (
                    liquid * filled * filled + 0.02
                )
                if step == 0:
                    moist = 0.05 + 0.4 * filled
                    energy_old[half, block, rows, :] = (
                        1.0 + 2.0 * moist
                    ) * warmth + 2.0 * moist * liquid
            return carry

        lax.fori_loop(0, ROWS // 8, body, 0)

    def pair_of(slot):
        upper = {M1: 1, M1X: 1, M2: 1, P1: 0, P1X: 0, P2: 0, W: 1 - core, X2: core}[slot]
        distance = {
            M1: 2, P1: 2, M2: 4, P2: 4, W: 1, X2: 3, M1X: 3 - 2 * core, P1X: 1 + 2 * core
        }[slot]
        first = me - (1 - upper) * distance
        valid = jnp.logical_and(first >= 0, first + distance < devices).astype(jnp.int32)
        pair = lax.rem(first + devices, devices) * PAIR_DEV + distance - 1
        return upper, pair, valid

    def lateral(step, half, slots, first):
        settings = []
        for slot in slots:
            upper, pair, valid = pair_of(slot)
            mine = couplings[1 - upper, pair]
            theirs = couplings[upper, pair]
            slope = jnp.full((8, LANES), upper.astype(jnp.float32) - 0.5 if not isinstance(upper, int) else upper - 0.5)
            mine = jnp.full((8, LANES), mine, jnp.int32) == 1
            theirs = jnp.full((8, LANES), theirs, jnp.int32) == 1
            live = jnp.full((8, LANES), valid, jnp.int32) == 1
            settings.append((slot, slope, mine, theirs, live))

        def body(tile, carry):
            rows = pl.ds(pl.multiple_of(tile * 8, 8), 8)
            heads = [own[message(step, half, 0), block, rows, :] for block in range(BLOCKS)]
            warmths = [own[message(step, half, 1), block, rows, :] for block in range(BLOCKS)]
            conds = [cond[half, block, rows, :] for block in range(BLOCKS)]
            zero = jnp.zeros((8, LANES), jnp.float32)
            if first:
                water = [zero, zero]
                heat = [zero, zero]
            else:
                water = [lat_water[half, block, rows, :] for block in range(BLOCKS)]
                heat = [lat_heat[half, block, rows, :] for block in range(BLOCKS)]
            for slot, slope, mine, theirs, live in settings:

                def far(field, at):
                    index = message(at, half, field)
                    return jnp.where(theirs, rx[slot, index, 1, rows, :], rx[slot, index, 0, rows, :])

                far_head, far_warmth, far_k = far(0, step), far(1, step), far(2, 0)
                filled = sig(far_head)
                far_cond = far_k * (sig(2.0 * far_warmth) * filled * filled + 0.02)
                near_head = jnp.where(mine, heads[1], heads[0])
                near_warmth = jnp.where(mine, warmths[1], warmths[0])
                near_cond = jnp.where(mine, conds[1], conds[0])
                flow = 0.25 * (near_cond + far_cond) * (near_head - far_head + slope)
                flow = jnp.where(live, flow, 0.0)
                carried = 2.0 * (
                    jnp.maximum(flow, 0.0) * near_warmth + jnp.minimum(flow, 0.0) * far_warmth
                )
                water[0] = water[0] - jnp.where(mine, 0.0, flow)
                water[1] = water[1] - jnp.where(mine, flow, 0.0)
                heat[0] = heat[0] - jnp.where(mine, 0.0, carried)
                heat[1] = heat[1] - jnp.where(mine, carried, 0.0)
            for block in range(BLOCKS):
                lat_water[half, block, rows, :] = water[block]
                lat_heat[half, block, rows, :] = heat[block]
            return carry

        lax.fori_loop(0, ROWS // 8, body, 0)

    sublane = lax.broadcasted_iota(jnp.int32, (BLOCKS, 8, LANES), 1)
    is_top = sublane == 0

    def new_head(step, half, row):
        if step == 0:
            return own[message(1, half, 0), :, strided(row), :]
        return result[half, 0, :, strided(row), :]

    def water(step, half):
        index = message(step, half, 0)

        def cond_row(row):
            return cond[half, :, strided(row), :]

        def head_row(row):
            return own[index, :, strided(row), :]

        def one(row, k_above, q_above, k_below, q_below, carry):
            filled = sat[step, half, :, strided(row), :]
            source = lat_water[half, :, strided(row), :] + q_above - q_below
            if step > 0:
                source = source - 0.8 * (filled - sat[0, half, :, strided(row), :])
            main = 0.8 * filled * (1.0 - filled) + 0.02 + k_above + k_below
            return forward_row(row, coef, main, k_above, k_below, source, carry)

        zero = jnp.zeros((BLOCKS, 8, LANES), jnp.float32)
        cond_first, head_first = cond_row(0), head_row(0)
        k_first = jnp.where(is_top, 0.0, 0.5 * (down(cond_row(CHUNK - 1)) + cond_first))
        q_first = -k_first * (head_first - down(head_row(CHUNK - 1)) - 1.0)

        def body(row, carry):
            cond_here, head_here, k_above, q_above, *chain = carry
            cond_next, head_next = cond_row(row + 1), head_row(row + 1)
            k_below = 0.5 * (cond_here + cond_next)
            q_below = -k_below * (head_next - head_here - 1.0)
            chain = one(row, k_above, q_above, k_below, q_below, chain)
            return (cond_next, head_next, k_below, q_below, *chain)

        start = (cond_first, head_first, k_first, q_first, zero, zero - 1.0, zero)
        _, _, k_above, q_above, *chain = lax.fori_loop(0, CHUNK - 1, body, start, unroll=True)
        last = one(CHUNK - 1, k_above, q_above, up(k_first), up(q_first), chain)

        def write(row, change):
            value = head_row(row) + change
            if step == 0:
                own[message(1, half, 0), :, strided(row), :] = value
            else:
                result[half, 0, :, strided(row), :] = value

        finish(coef, last, write)

    def energy(step, half):
        index = message(step, half, 1)

        def warmth_row(row):
            return own[index, :, strided(row), :]

        def passing_row(row):
            return lam[half, :, strided(row), :] * (1.5 - 0.5 * melt[half, :, strided(row), :])

        def one(row, here, extra, k_above, q_above, k_below, q_below, carry):
            moist = 0.05 + 0.4 * sig(new_head(step, half, row))
            liquid = melt[half, :, strided(row), :]
            slack = 1.0 + 2.0 * moist
            stored = slack * here + 2.0 * moist * liquid
            source = (
                lat_heat[half, :, strided(row), :]
                + q_above
                - q_below
                - 2.0 * (stored - energy_old[half, :, strided(row), :])
            )
            main = 2.0 * (slack + 4.0 * moist * liquid * (1.0 - liquid)) + k_above + k_below
            if extra is not None:
                main = main + extra
            return forward_row(row, coef, main, k_above, k_below, source, carry)

        zero = jnp.zeros((BLOCKS, 8, LANES), jnp.float32)
        passing_first, warmth_first = passing_row(0), warmth_row(0)
        top = jnp.stack(
            [
                jnp.broadcast_to(top_ref[pl.ds(block * HALVES + half, 1), :], (8, LANES))
                for block in range(BLOCKS)
            ]
        )
        k_first = jnp.where(is_top, 0.0, 0.5 * (down(passing_row(CHUNK - 1)) + passing_first))
        q_first = -k_first * (warmth_first - down(warmth_row(CHUNK - 1)))
        surface = jnp.where(is_top, 2.0 * passing_first, 0.0)
        q_surface = q_first + surface * (top - warmth_first)

        def body(row, carry):
            passing_here, warmth_here, extra, k_above, q_above, *chain = carry
            passing_next, warmth_next = passing_row(row + 1), warmth_row(row + 1)
            k_below = 0.5 * (passing_here + passing_next)
            q_below = -k_below * (warmth_next - warmth_here)
            chain = one(row, warmth_here, extra, k_above, q_above, k_below, q_below, chain)
            return (passing_next, warmth_next, zero, k_below, q_below, *chain)

        start = (passing_first, warmth_first, surface, k_first, q_surface, zero, zero - 1.0, zero)
        _, here, _, k_above, q_above, *chain = lax.fori_loop(0, CHUNK - 1, body, start, unroll=True)
        last = one(CHUNK - 1, here, None, k_above, q_above, up(k_first), up(q_first), chain)

        def write(row, change):
            value = warmth_row(row) + change
            if step == 0:
                own[message(1, half, 1), :, strided(row), :] = value
            else:
                result[half, 1, :, strided(row), :] = value

        finish(coef, last, write)

    def send_own(index):
        for slot in (P1, M1, W):
            copy(slot, index).start()

    def relay(index):
        copy(P1, index).wait_recv()
        copy(P2, index).start()
        copy(P1X, index).start()
        copy(M1, index).wait_recv()
        copy(M2, index).start()
        copy(M1X, index).start()

    def forward(index):
        copy(P2, index).wait_recv()
        copy(M2, index).wait_recv()
        copy(X2, index).start()

    def arrived(slot, indices):
        for index in indices:
            copy(slot, index).wait_recv()

    def first_sends(half):
        for field in range(2):
            for block in range(BLOCKS):
                load(half, field, block).wait()
            send_own(message(0, half, field))
        for block in range(BLOCKS):
            load(half, 2, block).wait()
        lookups(half)
        send_own(message(0, half, 2))

    def indices_of(step, half):
        return [message(step, half, field) for field in range(3 if step == 0 else 2)]

    def near(step, half):
        indices = indices_of(step, half)
        for index in indices:
            relay(index)

    def rest(step, half):
        indices = indices_of(step, half)
        arrived(W, indices)
        lateral(step, half, (W, P1, M1), True)
        for index in indices:
            forward(index)
        arrived(P1X, indices)
        arrived(M1X, indices)
        lateral(step, half, (P1X, M1X, P2, M2), False)
        arrived(X2, indices)
        lateral(step, half, (X2,), False)
        water(step, half)
        energy(step, half)

    for half in range(HALVES):
        for field in range(3):
            for block in range(BLOCKS):
                load(half, field, block).start()

    barrier = pltpu.get_barrier_semaphore()
    for device in (other, ahead, behind):
        pl.semaphore_signal(barrier, inc=1, device_id=(device,), device_id_type=MESH)
    pl.semaphore_wait(barrier, 3)

    first_sends(0)
    prepare(0, 0)
    near(0, 0)
    first_sends(1)
    prepare(0, 1)
    rest(0, 0)
    near(0, 1)
    for index in indices_of(1, 0):
        send_own(index)
    prepare(1, 0)
    rest(0, 1)
    near(1, 0)
    for index in indices_of(1, 1):
        send_own(index)
    prepare(1, 1)
    rest(1, 0)
    for field in range(2):
        for block in range(BLOCKS):
            store(0, field, block).start()
    near(1, 1)
    rest(1, 1)
    for field in range(2):
        for block in range(BLOCKS):
            store(1, field, block).start()
    for slot in range(SLOTS):
        for index in range(MESSAGES):
            copy(slot, index).wait_send()
    for half in range(HALVES):
        for field in range(2):
            for block in range(BLOCKS):
                store(half, field, block).wait()


def solution(mesh):
    devices = mesh.shape["cols"]

    def on_device(head, warmth, kinds, top, couplings, k_sat, heat_cond):
        plane = (BLOCKS, ROWS, LANES)
        anywhere = pl.BlockSpec(memory_space=pl.ANY)
        vector = pl.BlockSpec(memory_space=pltpu.VMEM)
        scalar = pl.BlockSpec(memory_space=pltpu.SMEM)
        f32 = jnp.float32
        out = jax.ShapeDtypeStruct(head.shape, f32)
        return pl.pallas_call(
            functools.partial(kernel, devices),
            out_shape=(out, out),
            in_specs=[anywhere, anywhere, anywhere, vector, scalar, scalar, scalar],
            out_specs=(anywhere, anywhere),
            scratch_shapes=[
                pltpu.VMEM((MESSAGES,) + plane, f32),
                pltpu.VMEM((SLOTS, MESSAGES) + plane, f32),
                pltpu.VMEM((HALVES, 2) + plane, f32),
                pltpu.VMEM((HALVES,) + plane, jnp.int32),
                pltpu.VMEM((HALVES,) + plane, f32),
                pltpu.VMEM((2, HALVES) + plane, f32),
                pltpu.VMEM((HALVES,) + plane, f32),
                pltpu.VMEM((HALVES,) + plane, f32),
                pltpu.VMEM((HALVES,) + plane, f32),
                pltpu.VMEM((HALVES,) + plane, f32),
                pltpu.VMEM((HALVES,) + plane, f32),
                pltpu.VMEM((CHUNK, BLOCKS, 8, LANES), f32),
                pltpu.VMEM((CHUNK, BLOCKS, 8, LANES), f32),
                pltpu.VMEM((CHUNK, BLOCKS, 8, LANES), f32),
                pltpu.SemaphoreType.DMA((HALVES, 3, BLOCKS)),
                pltpu.SemaphoreType.DMA((HALVES, 2, BLOCKS)),
                pltpu.SemaphoreType.DMA((SLOTS, MESSAGES)),
                pltpu.SemaphoreType.DMA((SLOTS, MESSAGES)),
            ],
            compiler_params=pltpu.CompilerParams(
                collective_id=0, has_side_effects=True, vmem_limit_bytes=32 * 1024 * 1024
            ),
        )(head, warmth, kinds, top.reshape(BLOCKS * HALVES, LANES), couplings, k_sat, heat_cond)

    placed = (P(None, "cols"), P(None, "cols"), P(None, "cols"), P("cols"), P(), P(), P())
    return jax.shard_map(
        on_device,
        mesh=mesh,
        in_specs=placed,
        out_specs=(P(None, "cols"), P(None, "cols")),
        check_vma=False,
    )
```

profile of v0, /device:TPU:1, one launch (start us, length us, event | category | flops | bytes accessed | tf_op | source)
XLA Modules:
  0.0 86.2 jit_solution(11152846313993767009)
XLA Ops:
  0.6 0.0 copy-start.6
  0.6 0.0 copy-start.5
  0.7 0.6 copy-done.6
  1.3 0.0 copy-done.5
  1.3 0.0 copy-start
  1.3 0.9 %copy-done = f32[128,512]{1,0:T(8,128)S(1)} copy-done((f32[128,512]{1,0:T(8,128)S(1)}, f32[128,512]{1,0:T(8,128)}, u32[]{:S(2)}) %copy-start) | copy-done | bytes 262168
  2.3 0.0 copy-start.1
  2.3 0.9 %copy-done.1 = f32[128,512]{1,0:T(8,128)S(1)} copy-done((f32[128,512]{1,0:T(8,128)S(1)}, f32[128,512]{1,0:T(8,128)}, u32[]{:S(2)}) %copy-start.1) | copy-done | bytes 262168
  3.2 0.0 copy-start.2
  3.2 0.9 %copy-done.2 = s32[128,512]{1,0:T(8,128)S(1)} copy-done((s32[128,512]{1,0:T(8,128)S(1)}, s32[128,512]{1,0:T(8,128)}, u32[]{:S(2)}) %copy-start.2) | copy-done | bytes 262168
  4.2 0.0 copy-start.3
  4.2 0.7 copy-done.3
  4.8 0.0 copy-start.4
  4.8 0.7 copy-done.4
  5.5 79.3 %shard_map.86 = (f32[128,512]{1,0:T(8,128)S(1)}, f32[128,512]{1,0:T(8,128)S(1)}) custom-call(f32[128,512]{1,0:T(8,128)S(1)} %copy-done, f32[128,512]{1,0:T(8,128)S(1)} %copy-done.1, s32[128,512]{1,0:T(8,128)S(1)} %copy-done.2, f32[4,128]{1,0:T(4,128)S(1)} %bitcast.1, s32[2,512]{1,0:T(2,128)S(1)} %copy-done.3, f32[8]{0:T(128)S(1)} %copy-done.5, f32[8]{0:T(128)S(1)} %copy-done.6), custom_call_target="tpu_custom_call" | custom-call | tf_op jit(solution)/shard_map/pallas_call | solution.py:485
  84.8 0.7 copy.11
  85.5 0.7 copy.12
Async XLA Ops:
  0.6 0.7 copy-start.6
  0.6 0.7 copy-start.5
  1.3 0.9 %copy-start = (f32[128,512]{1,0:T(8,128)S(1)}, f32[128,512]{1,0:T(8,128)}, u32[]{:S(2)}) copy-start(f32[128,512]{1,0:T(8,128)} %head_hbm.1) | copy-start | bytes 786436
  2.3 0.9 %copy-start.1 = (f32[128,512]{1,0:T(8,128)S(1)}, f32[128,512]{1,0:T(8,128)}, u32[]{:S(2)}) copy-start(f32[128,512]{1,0:T(8,128)} %warmth_hbm.1) | copy-start | bytes 786436
  3.2 0.9 %copy-start.2 = (s32[128,512]{1,0:T(8,128)S(1)}, s32[128,512]{1,0:T(8,128)}, u32[]{:S(2)}) copy-start(s32[128,512]{1,0:T(8,128)} %class_hbm.1) | copy-start | bytes 786436
  4.2 0.7 copy-start.3
  4.8 0.7 copy-start.4
where the time goes:
time: 86.5 us; the launch traced here: 86.2 us
  Pallas kernels  79.3 us (92%)
  local copies, waits for them, and re-layouts  6.28 us (7%)
    pallas_call x1, Pallas kernels, on_device(): pl.pallas_call(functools.partial(kernel, devices), out_shape=(out, out),...  79.3 us
    unnamed x16, local copies, waits for them, and re-layouts  6.28 us

commit v1 on v0

--- a/solution.py
+++ b/solution.py
@@ -19,6 +19,8 @@
 
 W, P1, M1, P1X, M1X, P2, M2, X2 = range(8)
 SLOTS = 8
+P1B, M1B, Y2 = 8, 9, 10
+COPIES = 11
 MESSAGES = 10
 
 
@@ -132,6 +134,8 @@
     other = me + 1 - 2 * core
     ahead = lax.rem(me + 2, devices)
     behind = lax.rem(me + devices - 2, devices)
+    chips = devices // 2
+    chip = me // 2
     coef = (c_ref, a_ref, d_ref)
 
     def columns(half, block):
@@ -139,7 +143,7 @@
 
     def load(half, field, block):
         source = (head_hbm, warmth_hbm, class_hbm)[field]
-        target = classes.at[half, block] if field == 2 else own.at[message(0, half, field), block]
+        target = classes.at[half, block] if field == 2 else own.at[0, message(0, half, field), block]
         return pltpu.make_async_copy(
             source.at[:, columns(half, block)], target, load_sem.at[half, field, block]
         )
@@ -152,31 +156,111 @@
             store_sem.at[half, field, block],
         )
 
-    def copy(slot, index):
-        if slot in (W, P1, M1):
-            source = own.at[index]
-        elif slot in (P1X, P2):
-            source = rx.at[P1, index]
-        elif slot in (M1X, M2):
-            source = rx.at[M1, index]
+    def copy(kind, index):
+        if kind == W:
+            source, target, device = own.at[0, index], rx.at[W, index], other
+        elif kind in (P1, P1B):
+            block = int(kind == P1B)
+            source, target, device = own.at[1 - core, index, block], rx.at[P1, index, block], ahead
+        elif kind in (M1, M1B):
+            block = int(kind == M1B)
+            source, target, device = own.at[core, index, block], rx.at[M1, index, block], behind
+        elif kind == P1X:
+            source, target, device = rx.at[P1, index], rx.at[P1X, index], other
+        elif kind == M1X:
+            source, target, device = rx.at[M1, index], rx.at[M1X, index], other
+        elif kind == P2:
+            source, target, device = rx.at[P1, index, 0], rx.at[P2, index, 0], ahead
+        elif kind == M2:
+            source, target, device = rx.at[M1, index, 0], rx.at[M2, index, 0], behind
+        elif kind == Y2:
+            source = rx.at[M1 - core * (M1 - P1), index, 1]
+            target = rx.at[M2 - core * (M2 - P2), index, 1]
+            device = behind + core * (ahead - behind)
         else:
-            source = rx.at[M2 - core * (M2 - P2), index]
-        target = {P1: ahead, P2: ahead, M1: behind, M2: behind}.get(slot, other)
+            source, target, device = rx.at[M2 - core * (M2 - P2), index], rx.at[X2, index], other
         return pltpu.make_async_remote_copy(
             src_ref=source,
-            dst_ref=rx.at[slot, index],
-            send_sem=send_sem.at[slot, index],
-            recv_sem=recv_sem.at[slot, index],
-            device_id=(target,),
+            dst_ref=target,
+            send_sem=send_sem.at[kind, index],
+            recv_sem=recv_sem.at[kind, index],
+            device_id=(device,),
             device_id_type=MESH,
         )
+
+    far_two = core * (chip >= 2) + (1 - core) * (chip <= chips - 3)
+    far_two_other = (1 - core) * (chip >= 2) + core * (chip <= chips - 3)
+    below, above = chip >= 1, chip <= chips - 2
+    middle = jnp.logical_and(below, above)
+    sends = {
+        W: None, P1: above, P1B: above, M1: below, M1B: below, P1X: below, M1X: above,
+        P2: middle, M2: middle, Y2: middle, X2: far_two == 1,
+    }
+    receives = {
+        W: None, P1: below, P1B: below, M1: above, M1B: above, P1X: below, M1X: above,
+        P2: chip >= 2, M2: chip <= chips - 3, Y2: far_two == 1, X2: far_two_other == 1,
+    }
+
+    def guarded(condition, action):
+        if condition is None:
+            action()
+        else:
+            pl.when(condition)(action)
+
+    def start(kind, *indices):
+        def action():
+            for index in indices:
+                copy(kind, index).start()
+
+        guarded(sends[kind], action)
+
+    def arrive(kind, *indices):
+        def action():
+            for index in indices:
+                copy(kind, index).wait_recv()
+
+        guarded(receives[kind], action)
+
+    def order_of(device, side):
+        pair = (device - side * lax.min(device, 4)) * PAIR_DEV + 3
+        return couplings[side, pair]
+
+    def order(index):
+        swap = jnp.full((8, LANES), order_of(me, core), jnp.int32) == 1
+
+        def body(tile, carry):
+            rows = pl.ds(pl.multiple_of(tile * 8, 8), 8)
+            zeroth = own[0, index, 0, rows, :]
+            oneth = own[0, index, 1, rows, :]
+            own[1, index, 0, rows, :] = jnp.where(swap, oneth, zeroth)
+            own[1, index, 1, rows, :] = jnp.where(swap, zeroth, oneth)
+            return carry
+
+        lax.fori_loop(0, ROWS // 8, body, 0, unroll=4)
+
+    def clear():
+        missing = (
+            (chip < 1, (P1, P1X)), (chip < 2, (P2,)), (chip > chips - 2, (M1, M1X)), (chip > chips - 3, (M2,)),
+            (far_two_other == 0, (X2,)),
+        )
+        for condition, slots in missing:
+
+            def action(slots=slots):
+                def body(index, carry):
+                    for slot in slots:
+                        rx[slot, index] = jnp.zeros((BLOCKS, ROWS, LANES), jnp.float32)
+                    return carry
+
+                lax.fori_loop(0, MESSAGES, body, 0)
+
+            pl.when(condition)(action)
 
     def lookups(half):
         def body(tile, carry):
             rows = pl.ds(pl.multiple_of(tile * 8, 8), 8)
             for block in range(BLOCKS):
                 kinds = classes[half, block, rows, :]
-                own[message(0, half, 2), block, rows, :] = lookup(k_table, kinds)
+                own[0, message(0, half, 2), block, rows, :] = lookup(k_table, kinds)
                 lam[half, block, rows, :] = lookup(lam_table, kinds)
             return carry
 
@@ -186,13 +270,13 @@
         def body(tile, carry):
             rows = pl.ds(pl.multiple_of(tile * 8, 8), 8)
             for block in range(BLOCKS):
-                head = own[message(step, half, 0), block, rows, :]
-                warmth = own[message(step, half, 1), block, rows, :]
+                head = own[0, message(step, half, 0), block, rows, :]
+                warmth = own[0, message(step, half, 1), block, rows, :]
                 filled = sig(head)
                 liquid = sig(2.0 * warmth)
                 sat[step, half, block, rows, :] = filled
                 melt[half, block, rows, :] = liquid
-                cond[half, block, rows, :] = own[message(0, half, 2), block, rows, :] * (
+                cond[half, block, rows, :] = own[0, message(0, half, 2), block, rows, :] * (
                     liquid * filled * filled + 0.02
                 )
                 if step == 0:
@@ -209,17 +293,22 @@
         distance = {
             M1: 2, P1: 2, M2: 4, P2: 4, W: 1, X2: 3, M1X: 3 - 2 * core, P1X: 1 + 2 * core
         }[slot]
+        sender = me + (2 * upper - 1) * distance
         first = me - (1 - upper) * distance
         valid = jnp.logical_and(first >= 0, first + distance < devices).astype(jnp.int32)
         pair = lax.rem(first + devices, devices) * PAIR_DEV + distance - 1
-        return upper, pair, valid
+        ordered = {W: 0, P1: 1 - core, M1: core, P1X: core, M1X: 1 - core, P2: 1 - core, M2: core, X2: 0}[slot]
+        sender_core = lax.rem(sender + devices, 2)
+        sender = lax.min(lax.max(sender, 0), devices - 1)
+        swap = ordered * order_of(sender, sender_core)
+        return upper, pair, valid, swap
 
     def lateral(step, half, slots, first):
         settings = []
         for slot in slots:
-            upper, pair, valid = pair_of(slot)
+            upper, pair, valid, swap = pair_of(slot)
             mine = couplings[1 - upper, pair]
-            theirs = couplings[upper, pair]
+            theirs = couplings[upper, pair] + swap
             slope = jnp.full((8, LANES), upper.astype(jnp.float32) - 0.5 if not isinstance(upper, int) else upper - 0.5)
             mine = jnp.full((8, LANES), mine, jnp.int32) == 1
             theirs = jnp.full((8, LANES), theirs, jnp.int32) == 1
@@ -228,8 +317,8 @@
 
         def body(tile, carry):
             rows = pl.ds(pl.multiple_of(tile * 8, 8), 8)
-            heads = [own[message(step, half, 0), block, rows, :] for block in range(BLOCKS)]
-            warmths = [own[message(step, half, 1), block, rows, :] for block in range(BLOCKS)]
+            heads = [own[0, message(step, half, 0), block, rows, :] for block in range(BLOCKS)]
+            warmths = [own[0, message(step, half, 1), block, rows, :] for block in range(BLOCKS)]
             conds = [cond[half, block, rows, :] for block in range(BLOCKS)]
             zero = jnp.zeros((8, LANES), jnp.float32)
             if first:
@@ -271,7 +360,7 @@
 
     def new_head(step, half, row):
         if step == 0:
-            return own[message(1, half, 0), :, strided(row), :]
+            return own[0, message(1, half, 0), :, strided(row), :]
         return result[half, 0, :, strided(row), :]
 
     def water(step, half):
@@ -281,7 +370,7 @@
             return cond[half, :, strided(row), :]
 
         def head_row(row):
-            return own[index, :, strided(row), :]
+            return own[0, index, :, strided(row), :]
 
         def one(row, k_above, q_above, k_below, q_below, carry):
             filled = sat[step, half, :, strided(row), :]
@@ -311,7 +400,7 @@
         def write(row, change):
             value = head_row(row) + change
             if step == 0:
-                own[message(1, half, 0), :, strided(row), :] = value
+                own[0, message(1, half, 0), :, strided(row), :] = value
             else:
                 result[half, 0, :, strided(row), :] = value
 
@@ -321,7 +410,7 @@
         index = message(step, half, 1)
 
         def warmth_row(row):
-            return own[index, :, strided(row), :]
+            return own[0, index, :, strided(row), :]
 
         def passing_row(row):
             return lam[half, :, strided(row), :] * (1.5 - 0.5 * melt[half, :, strided(row), :])
@@ -370,32 +459,19 @@
         def write(row, change):
             value = warmth_row(row) + change
             if step == 0:
-                own[message(1, half, 1), :, strided(row), :] = value
+                own[0, message(1, half, 1), :, strided(row), :] = value
             else:
                 result[half, 1, :, strided(row), :] = value
 
         finish(coef, last, write)
 
     def send_own(index):
-        for slot in (P1, M1, W):
-            copy(slot, index).start()
-
-    def relay(index):
-        copy(P1, index).wait_recv()
-        copy(P2, index).start()
-        copy(P1X, index).start()
-        copy(M1, index).wait_recv()
-        copy(M2, index).start()
-        copy(M1X, index).start()
-
-    def forward(index):
-        copy(P2, index).wait_recv()
-        copy(M2, index).wait_recv()
-        copy(X2, index).start()
-
-    def arrived(slot, indices):
-        for index in indices:
-            copy(slot, index).wait_recv()
+        start(W, index)
+        order(index)
+        start(P1, index)
+        start(M1, index)
+        start(P1B, index)
+        start(M1B, index)
 
     def first_sends(half):
         for field in range(2):
@@ -410,24 +486,41 @@
     def indices_of(step, half):
         return [message(step, half, field) for field in range(3 if step == 0 else 2)]
 
-    def near(step, half):
+    def relay(step, half):
+        for index in indices_of(step, half):
+            arrive(P1, index)
+            start(P2, index)
+            arrive(M1, index)
+            start(M2, index)
+            arrive(P1B, index)
+            arrive(M1B, index)
+            start(Y2, index)
+            start(P1X, index)
+            start(M1X, index)
+
+    def early(step, half):
+        arrive(W, *indices_of(step, half))
+        lateral(step, half, (W, P1, M1), True)
+
+    def late(step, half):
         indices = indices_of(step, half)
+        arrive(P1X, *indices)
+        arrive(M1X, *indices)
+        lateral(step, half, (P1X, M1X), False)
         for index in indices:
-            relay(index)
-
-    def rest(step, half):
-        indices = indices_of(step, half)
-        arrived(W, indices)
-        lateral(step, half, (W, P1, M1), True)
-        for index in indices:
-            forward(index)
-        arrived(P1X, indices)
-        arrived(M1X, indices)
-        lateral(step, half, (P1X, M1X, P2, M2), False)
-        arrived(X2, indices)
+            arrive(P2, index)
+            arrive(M2, index)
+            arrive(Y2, index)
+            start(X2, index)
+        lateral(step, half, (P2, M2), False)
+        arrive(X2, *indices)
         lateral(step, half, (X2,), False)
         water(step, half)
         energy(step, half)
+
+    def second_sends(half):
+        for index in indices_of(1, half):
+            send_own(index)
 
     for half in range(HALVES):
         for field in range(3):
@@ -435,37 +528,52 @@
                 load(half, field, block).start()
 
     barrier = pltpu.get_barrier_semaphore()
-    for device in (other, ahead, behind):
-        pl.semaphore_signal(barrier, inc=1, device_id=(device,), device_id_type=MESH)
-    pl.semaphore_wait(barrier, 3)
+    pl.semaphore_signal(barrier, inc=1, device_id=(other,), device_id_type=MESH)
+
+    @pl.when(above)
+    def _():
+        pl.semaphore_signal(barrier, inc=1, device_id=(ahead,), device_id_type=MESH)
+
+    @pl.when(below)
+    def _():
+        pl.semaphore_signal(barrier, inc=1, device_id=(behind,), device_id_type=MESH)
+
+    pl.semaphore_wait(barrier, 1 + above.astype(jnp.int32) + below.astype(jnp.int32))
 
     first_sends(0)
     prepare(0, 0)
-    near(0, 0)
+    clear()
+    relay(0, 0)
     first_sends(1)
     prepare(0, 1)
-    rest(0, 0)
-    near(0, 1)
-    for index in indices_of(1, 0):
-        send_own(index)
+    early(0, 0)
+    late(0, 0)
+    second_sends(0)
+    relay(0, 1)
     prepare(1, 0)
-    rest(0, 1)
-    near(1, 0)
-    for index in indices_of(1, 1):
-        send_own(index)
+    early(0, 1)
+    relay(1, 0)
+    late(0, 1)
+    second_sends(1)
     prepare(1, 1)
-    rest(1, 0)
+    early(1, 0)
+    relay(1, 1)
+    late(1, 0)
     for field in range(2):
         for block in range(BLOCKS):
             store(0, field, block).start()
-    near(1, 1)
-    rest(1, 1)
+    early(1, 1)
+    late(1, 1)
     for field in range(2):
         for block in range(BLOCKS):
             store(1, field, block).start()
-    for slot in range(SLOTS):
-        for index in range(MESSAGES):
-            copy(slot, index).wait_send()
+    for kind in range(COPIES):
+
+        def action(kind=kind):
+            for index in range(MESSAGES):
+                copy(kind, index).wait_send()
+
+        guarded(sends[kind], action)
     for half in range(HALVES):
         for field in range(2):
             for block in range(BLOCKS):
@@ -478,6 +586,7 @@
     def on_device(head, warmth, kinds, top, couplings, k_sat, heat_cond):
         plane = (BLOCKS, ROWS, LANES)
         anywhere = pl.BlockSpec(memory_space=pl.ANY)
+        hbm = pl.BlockSpec(memory_space=pltpu.HBM)
         vector = pl.BlockSpec(memory_space=pltpu.VMEM)
         scalar = pl.BlockSpec(memory_space=pltpu.SMEM)
         f32 = jnp.float32
@@ -485,10 +594,10 @@
         return pl.pallas_call(
             functools.partial(kernel, devices),
             out_shape=(out, out),
-            in_specs=[anywhere, anywhere, anywhere, vector, scalar, scalar, scalar],
+            in_specs=[hbm, hbm, hbm, vector, scalar, scalar, scalar],
             out_specs=(anywhere, anywhere),
             scratch_shapes=[
-                pltpu.VMEM((MESSAGES,) + plane, f32),
+                pltpu.VMEM((2, MESSAGES) + plane, f32),
                 pltpu.VMEM((SLOTS, MESSAGES) + plane, f32),
                 pltpu.VMEM((HALVES, 2) + plane, f32),
                 pltpu.VMEM((HALVES,) + plane, jnp.int32),
@@ -504,11 +613,11 @@
                 pltpu.VMEM((CHUNK, BLOCKS, 8, LANES), f32),
                 pltpu.SemaphoreType.DMA((HALVES, 3, BLOCKS)),
                 pltpu.SemaphoreType.DMA((HALVES, 2, BLOCKS)),
-                pltpu.SemaphoreType.DMA((SLOTS, MESSAGES)),
-                pltpu.SemaphoreType.DMA((SLOTS, MESSAGES)),
+                pltpu.SemaphoreType.DMA((COPIES, MESSAGES)),
+                pltpu.SemaphoreType.DMA((COPIES, MESSAGES)),
             ],
             compiler_params=pltpu.CompilerParams(
-                collective_id=0, has_side_effects=True, vmem_limit_bytes=32 * 1024 * 1024
+                collective_id=0, has_side_effects=True, vmem_limit_bytes=67043328
             ),
         )(head, warmth, kinds, top.reshape(BLOCKS * HALVES, LANES), couplings, k_sat, heat_cond)
 

time: 86.5 us -> 73.5 us (0.85)
  the two profiles are of different devices: /device:TPU:1 before, /device:TPU:6 now
where the time goes in v1:
time: 73.5 us; the launch traced here: 72.8 us
  Pallas kernels  69.8 us (95%)
  local copies, waits for them, and re-layouts  2.42 us (3%)
    pallas_call x1, Pallas kernels, on_device(): pl.pallas_call(functools.partial(kernel, devices), out_shape=(out, out),...  69.8 us
    unnamed x4, local copies, waits for them, and re-layouts  2.42 us

profile of v1, /device:TPU:6, one launch (start us, length us, event | category | flops | bytes accessed | tf_op | source)
XLA Modules:
  0.0 72.8 jit_solution(2388317300835329144)
XLA Ops:
  0.6 69.8 %shard_map.86 = (f32[128,512]{1,0:T(8,128)}, f32[128,512]{1,0:T(8,128)}) custom-call(f32[128,512]{1,0:T(8,128)} %head_hbm.1, f32[128,512]{1,0:T(8,128)} %warmth_hbm.1, s32[128,512]{1,0:T(8,128)} %class_hbm.1, f32[4,128]{1,0:T(4,128)} %bitcast.1, s32[2,512]{1,0:T(2,128)} %couplings.1, f32[8]{0:T(128)} %k_table.1, f32[8]{0:T(128)} %lam_table.1), custom_call_target="tpu_custom_call" | custom-call | tf_op jit(solution)/shard_map/pallas_call | solution.py:594
  70.4 0.0 copy-start
  70.4 1.7 %copy.11 = f32[128,512]{1,0:T(8,128)} copy(f32[128,512]{1,0:T(8,128)} %get-tuple-element.4) | data formatting | bytes 524288
  72.1 0.0 copy-done
  72.1 0.7 copy.12
Async XLA Ops:
  70.4 1.7 %copy-start = (f32[128,512]{1,0:T(8,128)S(1)}, f32[128,512]{1,0:T(8,128)}, u32[]{:S(2)}) copy-start(f32[128,512]{1,0:T(8,128)} %get-tuple-element.5) | copy-start | bytes 786436

commit v2 on v1

--- a/solution.py
+++ b/solution.py
@@ -19,8 +19,9 @@
 
 W, P1, M1, P1X, M1X, P2, M2, X2 = range(8)
 SLOTS = 8
-P1B, M1B, Y2 = 8, 9, 10
-COPIES = 11
+P1B, M1B = 8, 9
+COPIES = 10
+NATURAL, UPWARD, DOWNWARD = range(3)
 MESSAGES = 10
 
 
@@ -104,14 +105,15 @@
     head_hbm,
     warmth_hbm,
     class_hbm,
-    top_ref,
-    couplings,
-    k_table,
-    lam_table,
+    top_hbm,
+    couplings_hbm,
+    k_hbm,
+    lam_hbm,
     head_out,
     warmth_out,
     own,
     rx,
+    passed,
     result,
     classes,
     lam,
@@ -124,6 +126,11 @@
     c_ref,
     a_ref,
     d_ref,
+    top_ref,
+    couplings,
+    k_table,
+    lam_table,
+    table_sem,
     load_sem,
     store_sem,
     send_sem,
@@ -134,6 +141,7 @@
     other = me + 1 - 2 * core
     ahead = lax.rem(me + 2, devices)
     behind = lax.rem(me + devices - 2, devices)
+    across = lax.rem(me + devices - 1 + 2 * core, devices)
     chips = devices // 2
     chip = me // 2
     coef = (c_ref, a_ref, d_ref)
@@ -143,7 +151,7 @@
 
     def load(half, field, block):
         source = (head_hbm, warmth_hbm, class_hbm)[field]
-        target = classes.at[half, block] if field == 2 else own.at[0, message(0, half, field), block]
+        target = classes.at[half, block] if field == 2 else own.at[NATURAL, message(0, half, field), block]
         return pltpu.make_async_copy(
             source.at[:, columns(half, block)], target, load_sem.at[half, field, block]
         )
@@ -158,13 +166,13 @@
 
     def copy(kind, index):
         if kind == W:
-            source, target, device = own.at[0, index], rx.at[W, index], other
+            source, target, device = own.at[NATURAL, index], rx.at[W, index], other
         elif kind in (P1, P1B):
             block = int(kind == P1B)
-            source, target, device = own.at[1 - core, index, block], rx.at[P1, index, block], ahead
+            source, target, device = own.at[UPWARD, index, block], rx.at[P1, index, block], ahead
         elif kind in (M1, M1B):
             block = int(kind == M1B)
-            source, target, device = own.at[core, index, block], rx.at[M1, index, block], behind
+            source, target, device = own.at[DOWNWARD, index, block], rx.at[M1, index, block], behind
         elif kind == P1X:
             source, target, device = rx.at[P1, index], rx.at[P1X, index], other
         elif kind == M1X:
@@ -173,12 +181,8 @@
             source, target, device = rx.at[P1, index, 0], rx.at[P2, index, 0], ahead
         elif kind == M2:
             source, target, device = rx.at[M1, index, 0], rx.at[M2, index, 0], behind
-        elif kind == Y2:
-            source = rx.at[M1 - core * (M1 - P1), index, 1]
-            target = rx.at[M2 - core * (M2 - P2), index, 1]
-            device = behind + core * (ahead - behind)
         else:
-            source, target, device = rx.at[M2 - core * (M2 - P2), index], rx.at[X2, index], other
+            source, target, device = passed.at[index], rx.at[X2, index, 0], across
         return pltpu.make_async_remote_copy(
             src_ref=source,
             dst_ref=target,
@@ -188,17 +192,17 @@
             device_id_type=MESH,
         )
 
-    far_two = core * (chip >= 2) + (1 - core) * (chip <= chips - 3)
-    far_two_other = (1 - core) * (chip >= 2) + core * (chip <= chips - 3)
+    far_across = core * (chip <= chips - 3) + (1 - core) * (chip >= 2)
+    near_across = core * (chip <= chips - 2) + (1 - core) * (chip >= 1)
     below, above = chip >= 1, chip <= chips - 2
     middle = jnp.logical_and(below, above)
     sends = {
         W: None, P1: above, P1B: above, M1: below, M1B: below, P1X: below, M1X: above,
-        P2: middle, M2: middle, Y2: middle, X2: far_two == 1,
+        P2: middle, M2: middle, X2: middle,
     }
     receives = {
         W: None, P1: below, P1B: below, M1: above, M1B: above, P1X: below, M1X: above,
-        P2: chip >= 2, M2: chip <= chips - 3, Y2: far_two == 1, X2: far_two_other == 1,
+        P2: chip >= 2, M2: chip <= chips - 3, X2: far_across == 1,
     }
 
     def guarded(condition, action):
@@ -222,18 +226,37 @@
         guarded(receives[kind], action)
 
     def order_of(device, side):
-        pair = (device - side * lax.min(device, 4)) * PAIR_DEV + 3
-        return couplings[side, pair]
+        first = device if side == 0 else lax.max(device - 4, 0)
+        return couplings[side, first * PAIR_DEV + 3]
+
+    def mask(value):
+        return jnp.full((8, LANES), value, jnp.int32) == 1
 
     def order(index):
-        swap = jnp.full((8, LANES), order_of(me, core), jnp.int32) == 1
+        swaps = [(UPWARD, mask(order_of(me, 0))), (DOWNWARD, mask(order_of(me, 1)))]
 
         def body(tile, carry):
             rows = pl.ds(pl.multiple_of(tile * 8, 8), 8)
-            zeroth = own[0, index, 0, rows, :]
-            oneth = own[0, index, 1, rows, :]
-            own[1, index, 0, rows, :] = jnp.where(swap, oneth, zeroth)
-            own[1, index, 1, rows, :] = jnp.where(swap, zeroth, oneth)
+            zeroth = own[NATURAL, index, 0, rows, :]
+            oneth = own[NATURAL, index, 1, rows, :]
+            for version, swap in swaps:
+                own[version, index, 0, rows, :] = jnp.where(swap, oneth, zeroth)
+                own[version, index, 1, rows, :] = jnp.where(swap, zeroth, oneth)
+            return carry
+
+        lax.fori_loop(0, ROWS // 8, body, 0, unroll=4)
+
+    def passing(index):
+        sender = lax.min(lax.max(me + 2 - 4 * core, 0), devices - 1)
+        first = lax.max(sender - 3 * (1 - core), 0)
+        swap = core * order_of(sender, 0) + (1 - core) * order_of(sender, 1)
+        chosen = couplings[1 - core, first * PAIR_DEV + 2] + swap
+        chosen = mask(chosen)
+        slot = M1 - core * (M1 - P1)
+
+        def body(tile, carry):
+            rows = pl.ds(pl.multiple_of(tile * 8, 8), 8)
+            passed[index, rows, :] = jnp.where(chosen, rx[slot, index, 1, rows, :], rx[slot, index, 0, rows, :])
             return carry
 
         lax.fori_loop(0, ROWS // 8, body, 0, unroll=4)
@@ -241,7 +264,7 @@
     def clear():
         missing = (
             (chip < 1, (P1, P1X)), (chip < 2, (P2,)), (chip > chips - 2, (M1, M1X)), (chip > chips - 3, (M2,)),
-            (far_two_other == 0, (X2,)),
+            (far_across == 0, (X2,)),
         )
         for condition, slots in missing:
 
@@ -260,7 +283,7 @@
             rows = pl.ds(pl.multiple_of(tile * 8, 8), 8)
             for block in range(BLOCKS):
                 kinds = classes[half, block, rows, :]
-                own[0, message(0, half, 2), block, rows, :] = lookup(k_table, kinds)
+                own[NATURAL, message(0, half, 2), block, rows, :] = lookup(k_table, kinds)
                 lam[half, block, rows, :] = lookup(lam_table, kinds)
             return carry
 
@@ -270,13 +293,13 @@
         def body(tile, carry):
             rows = pl.ds(pl.multiple_of(tile * 8, 8), 8)
             for block in range(BLOCKS):
-                head = own[0, message(step, half, 0), block, rows, :]
-                warmth = own[0, message(step, half, 1), block, rows, :]
+                head = own[NATURAL, message(step, half, 0), block, rows, :]
+                warmth = own[NATURAL, message(step, half, 1), block, rows, :]
                 filled = sig(head)
                 liquid = sig(2.0 * warmth)
                 sat[step, half, block, rows, :] = filled
                 melt[half, block, rows, :] = liquid
-                cond[half, block, rows, :] = own[0, message(0, half, 2), block, rows, :] * (
+                cond[half, block, rows, :] = own[NATURAL, message(0, half, 2), block, rows, :] * (
                     liquid * filled * filled + 0.02
                 )
                 if step == 0:
@@ -297,10 +320,8 @@
         first = me - (1 - upper) * distance
         valid = jnp.logical_and(first >= 0, first + distance < devices).astype(jnp.int32)
         pair = lax.rem(first + devices, devices) * PAIR_DEV + distance - 1
-        ordered = {W: 0, P1: 1 - core, M1: core, P1X: core, M1X: 1 - core, P2: 1 - core, M2: core, X2: 0}[slot]
-        sender_core = lax.rem(sender + devices, 2)
         sender = lax.min(lax.max(sender, 0), devices - 1)
-        swap = ordered * order_of(sender, sender_core)
+        swap = order_of(sender, upper) if isinstance(upper, int) else 0
         return upper, pair, valid, swap
 
     def lateral(step, half, slots, first):
@@ -310,15 +331,12 @@
             mine = couplings[1 - upper, pair]
             theirs = couplings[upper, pair] + swap
             slope = jnp.full((8, LANES), upper.astype(jnp.float32) - 0.5 if not isinstance(upper, int) else upper - 0.5)
-            mine = jnp.full((8, LANES), mine, jnp.int32) == 1
-            theirs = jnp.full((8, LANES), theirs, jnp.int32) == 1
-            live = jnp.full((8, LANES), valid, jnp.int32) == 1
-            settings.append((slot, slope, mine, theirs, live))
+            settings.append((slot, slope, mask(mine), mask(theirs), mask(valid)))
 
         def body(tile, carry):
             rows = pl.ds(pl.multiple_of(tile * 8, 8), 8)
-            heads = [own[0, message(step, half, 0), block, rows, :] for block in range(BLOCKS)]
-            warmths = [own[0, message(step, half, 1), block, rows, :] for block in range(BLOCKS)]
+            heads = [own[NATURAL, message(step, half, 0), block, rows, :] for block in range(BLOCKS)]
+            warmths = [own[NATURAL, message(step, half, 1), block, rows, :] for block in range(BLOCKS)]
             conds = [cond[half, block, rows, :] for block in range(BLOCKS)]
             zero = jnp.zeros((8, LANES), jnp.float32)
             if first:
@@ -331,6 +349,8 @@
 
                 def far(field, at):
                     index = message(at, half, field)
+                    if slot in (P2, M2, X2):
+                        return rx[slot, index, 0, rows, :]
                     return jnp.where(theirs, rx[slot, index, 1, rows, :], rx[slot, index, 0, rows, :])
 
                 far_head, far_warmth, far_k = far(0, step), far(1, step), far(2, 0)
@@ -360,7 +380,7 @@
 
     def new_head(step, half, row):
         if step == 0:
-            return own[0, message(1, half, 0), :, strided(row), :]
+            return own[NATURAL, message(1, half, 0), :, strided(row), :]
         return result[half, 0, :, strided(row), :]
 
     def water(step, half):
@@ -370,7 +390,7 @@
             return cond[half, :, strided(row), :]
 
         def head_row(row):
-            return own[0, index, :, strided(row), :]
+            return own[NATURAL, index, :, strided(row), :]
 
         def one(row, k_above, q_above, k_below, q_below, carry):
             filled = sat[step, half, :, strided(row), :]
@@ -400,7 +420,7 @@
         def write(row, change):
             value = head_row(row) + change
             if step == 0:
-                own[0, message(1, half, 0), :, strided(row), :] = value
+                own[NATURAL, message(1, half, 0), :, strided(row), :] = value
             else:
                 result[half, 0, :, strided(row), :] = value
 
@@ -410,7 +430,7 @@
         index = message(step, half, 1)
 
         def warmth_row(row):
-            return own[0, index, :, strided(row), :]
+            return own[NATURAL, index, :, strided(row), :]
 
         def passing_row(row):
             return lam[half, :, strided(row), :] * (1.5 - 0.5 * melt[half, :, strided(row), :])
@@ -459,7 +479,7 @@
         def write(row, change):
             value = warmth_row(row) + change
             if step == 0:
-                own[0, message(1, half, 1), :, strided(row), :] = value
+                own[NATURAL, message(1, half, 1), :, strided(row), :] = value
             else:
                 result[half, 1, :, strided(row), :] = value
 
@@ -486,17 +506,18 @@
     def indices_of(step, half):
         return [message(step, half, field) for field in range(3 if step == 0 else 2)]
 
-    def relay(step, half):
-        for index in indices_of(step, half):
+    def relay(step, half, fields=(0, 1, 2)):
+        for index in [message(step, half, field) for field in fields if step == 0 or field < 2]:
             arrive(P1, index)
             start(P2, index)
             arrive(M1, index)
             start(M2, index)
             arrive(P1B, index)
             arrive(M1B, index)
-            start(Y2, index)
+            passing(index)
             start(P1X, index)
             start(M1X, index)
+            start(X2, index)
 
     def early(step, half):
         arrive(W, *indices_of(step, half))
@@ -507,39 +528,50 @@
         arrive(P1X, *indices)
         arrive(M1X, *indices)
         lateral(step, half, (P1X, M1X), False)
-        for index in indices:
-            arrive(P2, index)
-            arrive(M2, index)
-            arrive(Y2, index)
-            start(X2, index)
-        lateral(step, half, (P2, M2), False)
+        arrive(P2, *indices)
+        arrive(M2, *indices)
         arrive(X2, *indices)
-        lateral(step, half, (X2,), False)
+        lateral(step, half, (P2, M2, X2), False)
+
+    def solve(step, half, send=False):
         water(step, half)
+        if send:
+            send_own(message(1, half, 0))
         energy(step, half)
-
-    def second_sends(half):
-        for index in indices_of(1, half):
-            send_own(index)
+        if send:
+            send_own(message(1, half, 1))
+
+    barrier = pltpu.get_barrier_semaphore()
+    pl.semaphore_signal(barrier, inc=1, device_id=(other,), device_id_type=MESH)
+
+    @pl.when(above)
+    def _():
+        pl.semaphore_signal(barrier, inc=1, device_id=(ahead,), device_id_type=MESH)
+
+    @pl.when(below)
+    def _():
+        pl.semaphore_signal(barrier, inc=1, device_id=(behind,), device_id_type=MESH)
+
+    @pl.when(near_across == 1)
+    def _():
+        pl.semaphore_signal(barrier, inc=1, device_id=(across,), device_id_type=MESH)
 
     for half in range(HALVES):
         for field in range(3):
             for block in range(BLOCKS):
                 load(half, field, block).start()
-
-    barrier = pltpu.get_barrier_semaphore()
-    pl.semaphore_signal(barrier, inc=1, device_id=(other,), device_id_type=MESH)
-
-    @pl.when(above)
-    def _():
-        pl.semaphore_signal(barrier, inc=1, device_id=(ahead,), device_id_type=MESH)
-
-    @pl.when(below)
-    def _():
-        pl.semaphore_signal(barrier, inc=1, device_id=(behind,), device_id_type=MESH)
-
-    pl.semaphore_wait(barrier, 1 + above.astype(jnp.int32) + below.astype(jnp.int32))
-
+    tables = [
+        pltpu.make_async_copy(source, target, table_sem.at[place])
+        for place, (source, target) in enumerate(
+            ((couplings_hbm, couplings), (k_hbm, k_table), (lam_hbm, lam_table), (top_hbm, top_ref))
+        )
+    ]
+    for table in tables:
+        table.start()
+    pl.semaphore_wait(barrier, 1 + above.astype(jnp.int32) + below.astype(jnp.int32) + near_across)
+
+    for table in tables:
+        table.wait()
     first_sends(0)
     prepare(0, 0)
     clear()
@@ -548,22 +580,28 @@
     prepare(0, 1)
     early(0, 0)
     late(0, 0)
-    second_sends(0)
+    water(0, 0)
+    energy(0, 0)
     relay(0, 1)
+    send_own(message(1, 0, 0))
+    send_own(message(1, 0, 1))
     prepare(1, 0)
     early(0, 1)
-    relay(1, 0)
     late(0, 1)
-    second_sends(1)
+    relay(1, 0, (0,))
+    solve(0, 1, True)
+    relay(1, 0, (1,))
     prepare(1, 1)
     early(1, 0)
     relay(1, 1)
     late(1, 0)
+    solve(1, 0)
     for field in range(2):
         for block in range(BLOCKS):
             store(0, field, block).start()
     early(1, 1)
     late(1, 1)
+    solve(1, 1)
     for field in range(2):
         for block in range(BLOCKS):
             store(1, field, block).start()
@@ -587,18 +625,17 @@
         plane = (BLOCKS, ROWS, LANES)
         anywhere = pl.BlockSpec(memory_space=pl.ANY)
         hbm = pl.BlockSpec(memory_space=pltpu.HBM)
-        vector = pl.BlockSpec(memory_space=pltpu.VMEM)
-        scalar = pl.BlockSpec(memory_space=pltpu.SMEM)
         f32 = jnp.float32
         out = jax.ShapeDtypeStruct(head.shape, f32)
         return pl.pallas_call(
             functools.partial(kernel, devices),
             out_shape=(out, out),
-            in_specs=[hbm, hbm, hbm, vector, scalar, scalar, scalar],
+            in_specs=[hbm] * 7,
             out_specs=(anywhere, anywhere),
             scratch_shapes=[
-                pltpu.VMEM((2, MESSAGES) + plane, f32),
+                pltpu.VMEM((3, MESSAGES) + plane, f32),
                 pltpu.VMEM((SLOTS, MESSAGES) + plane, f32),
+                pltpu.VMEM((MESSAGES, ROWS, LANES), f32),
                 pltpu.VMEM((HALVES, 2) + plane, f32),
                 pltpu.VMEM((HALVES,) + plane, jnp.int32),
                 pltpu.VMEM((HALVES,) + plane, f32),
@@ -611,6 +648,11 @@
                 pltpu.VMEM((CHUNK, BLOCKS, 8, LANES), f32),
                 pltpu.VMEM((CHUNK, BLOCKS, 8, LANES), f32),
                 pltpu.VMEM((CHUNK, BLOCKS, 8, LANES), f32),
+                pltpu.VMEM((BLOCKS * HALVES, LANES), f32),
+                pltpu.SMEM(couplings.shape, jnp.int32),
+                pltpu.SMEM(k_sat.shape, f32),
+                pltpu.SMEM(heat_cond.shape, f32),
+                pltpu.SemaphoreType.DMA((4,)),
                 pltpu.SemaphoreType.DMA((HALVES, 3, BLOCKS)),
                 pltpu.SemaphoreType.DMA((HALVES, 2, BLOCKS)),
                 pltpu.SemaphoreType.DMA((COPIES, MESSAGES)),

time: 73.5 us -> 68.5 us (0.932)
  Pallas kernels: 69.8 us -> 65.2 us
    pallas_call x1, Pallas kernels: 69.8 us -> 65.2 us  [on_device(): pl.pallas_call(functools.partial(kernel, devices), out_shape=(out, out),...]
where the time goes in v2:
time: 68.5 us; the launch traced here: 68.3 us
  Pallas kernels  65.2 us (95%)
  local copies, waits for them, and re-layouts  2.42 us (4%)
    pallas_call x1, Pallas kernels, on_device(): pl.pallas_call(functools.partial(kernel, devices), out_shape=(out, out),...  65.2 us
    unnamed x4, local copies, waits for them, and re-layouts  2.42 us

profile of v2, /device:TPU:6, one launch (start us, length us, event | category | flops | bytes accessed | tf_op | source)
XLA Modules:
  0.0 68.3 jit_solution(17121958333521170457)
XLA Ops:
  0.6 65.2 %shard_map.86 = (f32[128,512]{1,0:T(8,128)}, f32[128,512]{1,0:T(8,128)}) custom-call(f32[128,512]{1,0:T(8,128)} %head_hbm.1, f32[128,512]{1,0:T(8,128)} %warmth_hbm.1, s32[128,512]{1,0:T(8,128)} %class_hbm.1, f32[4,128]{1,0:T(4,128)} %bitcast.1, s32[2,512]{1,0:T(2,128)} %couplings_hbm.1, f32[8]{0:T(128)} %k_hbm.1, f32[8]{0:T(128)} %lam_hbm.1), custom_call_target="tpu_custom_call" | custom-call | tf_op jit(solution)/shard_map/pallas_call | solution.py:630
  65.9 0.0 copy-start
  65.9 1.7 %copy.11 = f32[128,512]{1,0:T(8,128)} copy(f32[128,512]{1,0:T(8,128)} %get-tuple-element.4) | data formatting | bytes 524288
  67.6 0.0 copy-done
  67.6 0.7 %copy.12 = f32[128,512]{1,0:T(8,128)} copy(f32[128,512]{1,0:T(8,128)S(1)} %copy-done) | data formatting | bytes 524288
Async XLA Ops:
  65.9 1.7 %copy-start = (f32[128,512]{1,0:T(8,128)S(1)}, f32[128,512]{1,0:T(8,128)}, u32[]{:S(2)}) copy-start(f32[128,512]{1,0:T(8,128)} %get-tuple-element.5) | copy-start | bytes 786436

commit v3 on v2

--- a/solution.py
+++ b/solution.py
@@ -109,8 +109,8 @@
     couplings_hbm,
     k_hbm,
     lam_hbm,
-    head_out,
-    warmth_out,
+    base_out,
+    change_out,
     own,
     rx,
     passed,
@@ -133,6 +133,7 @@
     table_sem,
     load_sem,
     store_sem,
+    base_sem,
     send_sem,
     recv_sem,
 ):
@@ -157,11 +158,17 @@
         )
 
     def store(half, field, block):
-        target = (head_out, warmth_out)[field]
         return pltpu.make_async_copy(
             result.at[half, field, block],
-            target.at[:, columns(half, block)],
+            change_out.at[field, :, columns(half, block)],
             store_sem.at[half, field, block],
+        )
+
+    def store_base(half, field, block):
+        return pltpu.make_async_copy(
+            own.at[NATURAL, message(1, half, field), block],
+            base_out.at[field, :, columns(half, block)],
+            base_sem.at[half, field, block],
         )
 
     def copy(kind, index):
@@ -381,7 +388,7 @@
     def new_head(step, half, row):
         if step == 0:
             return own[NATURAL, message(1, half, 0), :, strided(row), :]
-        return result[half, 0, :, strided(row), :]
+        return own[NATURAL, message(1, half, 0), :, strided(row), :] + result[half, 0, :, strided(row), :]
 
     def water(step, half):
         index = message(step, half, 0)
@@ -418,11 +425,10 @@
         last = one(CHUNK - 1, k_above, q_above, up(k_first), up(q_first), chain)
 
         def write(row, change):
-            value = head_row(row) + change
             if step == 0:
-                own[NATURAL, message(1, half, 0), :, strided(row), :] = value
+                own[NATURAL, message(1, half, 0), :, strided(row), :] = head_row(row) + change
             else:
-                result[half, 0, :, strided(row), :] = value
+                result[half, 0, :, strided(row), :] = change
 
         finish(coef, last, write)
 
@@ -477,11 +483,10 @@
         last = one(CHUNK - 1, here, None, k_above, q_above, up(k_first), up(q_first), chain)
 
         def write(row, change):
-            value = warmth_row(row) + change
             if step == 0:
-                own[NATURAL, message(1, half, 1), :, strided(row), :] = value
+                own[NATURAL, message(1, half, 1), :, strided(row), :] = warmth_row(row) + change
             else:
-                result[half, 1, :, strided(row), :] = value
+                result[half, 1, :, strided(row), :] = change
 
         finish(coef, last, write)
 
@@ -530,8 +535,9 @@
         lateral(step, half, (P1X, M1X), False)
         arrive(P2, *indices)
         arrive(M2, *indices)
+        lateral(step, half, (P2, M2), False)
         arrive(X2, *indices)
-        lateral(step, half, (P2, M2, X2), False)
+        lateral(step, half, (X2,), False)
 
     def solve(step, half, send=False):
         water(step, half)
@@ -556,17 +562,18 @@
     def _():
         pl.semaphore_signal(barrier, inc=1, device_id=(across,), device_id_type=MESH)
 
-    for half in range(HALVES):
-        for field in range(3):
-            for block in range(BLOCKS):
-                load(half, field, block).start()
     tables = [
         pltpu.make_async_copy(source, target, table_sem.at[place])
         for place, (source, target) in enumerate(
             ((couplings_hbm, couplings), (k_hbm, k_table), (lam_hbm, lam_table), (top_hbm, top_ref))
         )
     ]
-    for table in tables:
+    tables[0].start()
+    for half in range(HALVES):
+        for field in range(3):
+            for block in range(BLOCKS):
+                load(half, field, block).start()
+    for table in tables[1:]:
         table.start()
     pl.semaphore_wait(barrier, 1 + above.astype(jnp.int32) + below.astype(jnp.int32) + near_across)
 
@@ -594,12 +601,14 @@
     prepare(1, 1)
     early(1, 0)
     relay(1, 1)
+    early(1, 1)
     late(1, 0)
     solve(1, 0)
     for field in range(2):
         for block in range(BLOCKS):
             store(0, field, block).start()
-    early(1, 1)
+            for half in range(HALVES):
+                store_base(half, field, block).start()
     late(1, 1)
     solve(1, 1)
     for field in range(2):
@@ -616,6 +625,7 @@
         for field in range(2):
             for block in range(BLOCKS):
                 store(half, field, block).wait()
+                store_base(half, field, block).wait()
 
 
 def solution(mesh):
@@ -623,15 +633,14 @@
 
     def on_device(head, warmth, kinds, top, couplings, k_sat, heat_cond):
         plane = (BLOCKS, ROWS, LANES)
-        anywhere = pl.BlockSpec(memory_space=pl.ANY)
         hbm = pl.BlockSpec(memory_space=pltpu.HBM)
         f32 = jnp.float32
-        out = jax.ShapeDtypeStruct(head.shape, f32)
-        return pl.pallas_call(
+        out = pltpu.VMEM((2,) + head.shape, f32)
+        base, change = pl.pallas_call(
             functools.partial(kernel, devices),
             out_shape=(out, out),
             in_specs=[hbm] * 7,
-            out_specs=(anywhere, anywhere),
+            out_specs=(pl.BlockSpec(memory_space=pltpu.VMEM),) * 2,
             scratch_shapes=[
                 pltpu.VMEM((3, MESSAGES) + plane, f32),
                 pltpu.VMEM((SLOTS, MESSAGES) + plane, f32),
@@ -655,13 +664,15 @@
                 pltpu.SemaphoreType.DMA((4,)),
                 pltpu.SemaphoreType.DMA((HALVES, 3, BLOCKS)),
                 pltpu.SemaphoreType.DMA((HALVES, 2, BLOCKS)),
+                pltpu.SemaphoreType.DMA((HALVES, 2, BLOCKS)),
                 pltpu.SemaphoreType.DMA((COPIES, MESSAGES)),
                 pltpu.SemaphoreType.DMA((COPIES, MESSAGES)),
             ],
             compiler_params=pltpu.CompilerParams(
-                collective_id=0, has_side_effects=True, vmem_limit_bytes=67043328
+                collective_id=0, has_side_effects=True, vmem_limit_bytes=65900000
             ),
         )(head, warmth, kinds, top.reshape(BLOCKS * HALVES, LANES), couplings, k_sat, heat_cond)
+        return base[0] + change[0], base[1] + change[1]
 
     placed = (P(None, "cols"), P(None, "cols"), P(None, "cols"), P("cols"), P(), P(), P())
     return jax.shard_map(

time: 68.5 us -> 66.4 us (0.969)
  local copies, waits for them, and re-layouts: 2.42 us -> 0 us
  other arithmetic: 0 us -> 0.87 us
    unnamed x4 -> x0, local copies, waits for them, and re-layouts: 2.42 us -> none
    add x0 -> x1, other arithmetic: none -> 0.87 us  [on_device(): return (base[0] + change[0], base[1] + change[1])]
where the time goes in v3:
time: 66.4 us; the launch traced here: 66.2 us
  Pallas kernels  64.7 us (97%)
  other arithmetic  0.87 us (1%)
    pallas_call x1, Pallas kernels, on_device(): pl.pallas_call(functools.partial(kernel, devices), out_shape=(out, out),...  64.7 us

profile of v3, /device:TPU:6, one launch (start us, length us, event | category | flops | bytes accessed | tf_op | source)
XLA Modules:
  0.0 66.2 jit_solution(12769083643050215322)
XLA Ops:
  0.6 64.7 %shard_map.86 = (f32[2,128,512]{2,1,0:T(8,128)S(1)}, f32[2,128,512]{2,1,0:T(8,128)S(1)}) custom-call(f32[128,512]{1,0:T(8,128)} %head_hbm.1, f32[128,512]{1,0:T(8,128)} %warmth_hbm.1, s32[128,512]{1,0:T(8,128)} %class_hbm.1, f32[4,128]{1,0:T(4,128)} %bitcast.5, s32[2,512]{1,0:T(2,128)} %couplings_hbm.1, f32[8]{0:T(128)} %k_hbm.1, f32[8]{0:T(128)} %lam_hbm.1), custom_call_target="tpu_custom_call" | custom-call | tf_op jit(solution)/shard_map/pallas_call | solution.py:639
  65.4 0.9 %add_bitcast_fusion = (f32[128,512]{1,0:T(8,128)}, f32[128,512]{1,0:T(8,128)}) fusion(f32[2,128,512]{2,1,0:T(8,128)S(1)} %get-tuple-element.5, f32[2,128,512]{2,1,0:T(8,128)S(1)} %get-tuple-element.4), kind=kLoop, calls=%fused_computation | loop fusion | flops 131072 | bytes 1572864 | tf_op jit(solution)/shard_map/add | solution.py:675

commit v4 on v3

--- a/solution.py
+++ b/solution.py
@@ -21,6 +21,8 @@
 SLOTS = 8
 P1B, M1B = 8, 9
 COPIES = 10
+SINGLE = (P1, P1B, M1, M1B)
+GROUPED = (W, P1X, M1X, P2, M2, X2)
 NATURAL, UPWARD, DOWNWARD = range(3)
 MESSAGES = 10
 
@@ -133,9 +135,9 @@
     table_sem,
     load_sem,
     store_sem,
-    base_sem,
     send_sem,
-    recv_sem,
+    single_sem,
+    group_sem,
 ):
     me = lax.axis_index("cols")
     core = lax.rem(me, 2)
@@ -154,21 +156,25 @@
         source = (head_hbm, warmth_hbm, class_hbm)[field]
         target = classes.at[half, block] if field == 2 else own.at[NATURAL, message(0, half, field), block]
         return pltpu.make_async_copy(
-            source.at[:, columns(half, block)], target, load_sem.at[half, field, block]
+            source.at[:, columns(half, block)], target, load_sem.at[half, field]
         )
+
+    def loaded(half, field):
+        ref = classes.at[half] if field == 2 else own.at[NATURAL, message(0, half, field)]
+        pltpu.make_async_copy(ref, ref, load_sem.at[half, field]).wait()
 
     def store(half, field, block):
         return pltpu.make_async_copy(
             result.at[half, field, block],
             change_out.at[field, :, columns(half, block)],
-            store_sem.at[half, field, block],
+            store_sem.at[0],
         )
 
     def store_base(half, field, block):
         return pltpu.make_async_copy(
             own.at[NATURAL, message(1, half, field), block],
             base_out.at[field, :, columns(half, block)],
-            base_sem.at[half, field, block],
+            store_sem.at[1],
         )
 
     def copy(kind, index):
@@ -193,10 +199,20 @@
         return pltpu.make_async_remote_copy(
             src_ref=source,
             dst_ref=target,
-            send_sem=send_sem.at[kind, index],
-            recv_sem=recv_sem.at[kind, index],
+            send_sem=send_sem.at[kind],
+            recv_sem=arrival_sem(kind, index),
             device_id=(device,),
             device_id_type=MESH,
+        )
+
+    def arrival_sem(kind, index):
+        if kind in SINGLE:
+            return single_sem.at[SINGLE.index(kind), index]
+        return group_sem.at[GROUPED.index(kind), index // 3 if index < 6 else index // 2 - 1]
+
+    def whole(kind, ref, arrival):
+        return pltpu.make_async_remote_copy(
+            src_ref=ref, dst_ref=ref, send_sem=send_sem.at[kind], recv_sem=arrival, device_id=(other,), device_id_type=MESH
         )
 
     far_across = core * (chip <= chips - 3) + (1 - core) * (chip >= 2)
@@ -227,8 +243,13 @@
 
     def arrive(kind, *indices):
         def action():
-            for index in indices:
-                copy(kind, index).wait_recv()
+            if kind in SINGLE:
+                for index in indices:
+                    copy(kind, index).wait_recv()
+            else:
+                span = pl.ds(indices[0], len(indices))
+                ref = rx.at[kind, span] if kind in (W, P1X, M1X) else rx.at[kind, span, 0]
+                whole(kind, ref, arrival_sem(kind, indices[0])).wait_recv()
 
         guarded(receives[kind], action)
 
@@ -500,11 +521,9 @@
 
     def first_sends(half):
         for field in range(2):
-            for block in range(BLOCKS):
-                load(half, field, block).wait()
+            loaded(half, field)
             send_own(message(0, half, field))
-        for block in range(BLOCKS):
-            load(half, 2, block).wait()
+        loaded(half, 2)
         lookups(half)
         send_own(message(0, half, 2))
 
@@ -617,15 +636,12 @@
     for kind in range(COPIES):
 
         def action(kind=kind):
-            for index in range(MESSAGES):
-                copy(kind, index).wait_send()
+            ref = rx.at[W] if kind in (W, P1X, M1X) else passed
+            whole(kind, ref, arrival_sem(kind, 0)).wait_send()
 
         guarded(sends[kind], action)
-    for half in range(HALVES):
-        for field in range(2):
-            for block in range(BLOCKS):
-                store(half, field, block).wait()
-                store_base(half, field, block).wait()
+    for place, ref in enumerate((result, own.at[NATURAL, pl.ds(6, 4)])):
+        pltpu.make_async_copy(ref, ref, store_sem.at[place]).wait()
 
 
 def solution(mesh):
@@ -662,11 +678,11 @@
                 pltpu.SMEM(k_sat.shape, f32),
                 pltpu.SMEM(heat_cond.shape, f32),
                 pltpu.SemaphoreType.DMA((4,)),
-                pltpu.SemaphoreType.DMA((HALVES, 3, BLOCKS)),
-                pltpu.SemaphoreType.DMA((HALVES, 2, BLOCKS)),
-                pltpu.SemaphoreType.DMA((HALVES, 2, BLOCKS)),
-                pltpu.SemaphoreType.DMA((COPIES, MESSAGES)),
-                pltpu.SemaphoreType.DMA((COPIES, MESSAGES)),
+                pltpu.SemaphoreType.DMA((HALVES, 3)),
+                pltpu.SemaphoreType.DMA((2,)),
+                pltpu.SemaphoreType.DMA((COPIES,)),
+                pltpu.SemaphoreType.DMA((len(SINGLE), MESSAGES)),
+                pltpu.SemaphoreType.DMA((len(GROUPED), 4)),
             ],
             compiler_params=pltpu.CompilerParams(
                 collective_id=0, has_side_effects=True, vmem_limit_bytes=65900000

time: 66.4 us -> 64.9 us (0.977)
  Pallas kernels: 64.7 us -> 63.3 us
    pallas_call x1, Pallas kernels: 64.7 us -> 63.3 us  [on_device(): pl.pallas_call(functools.partial(kernel, devices), out_shape=(out, out),...]
where the time goes in v4:
time: 64.9 us; the launch traced here: 64.8 us
  Pallas kernels  63.3 us (98%)
  other arithmetic  0.87 us (1%)
    pallas_call x1, Pallas kernels, on_device(): pl.pallas_call(functools.partial(kernel, devices), out_shape=(out, out),...  63.3 us

profile of v4, /device:TPU:6, one launch (start us, length us, event | category | flops | bytes accessed | tf_op | source)
XLA Modules:
  0.0 64.8 jit_solution(4054685458369318294)
XLA Ops:
  0.6 63.3 %shard_map.86 = (f32[2,128,512]{2,1,0:T(8,128)S(1)}, f32[2,128,512]{2,1,0:T(8,128)S(1)}) custom-call(f32[128,512]{1,0:T(8,128)} %head_hbm.1, f32[128,512]{1,0:T(8,128)} %warmth_hbm.1, s32[128,512]{1,0:T(8,128)} %class_hbm.1, f32[4,128]{1,0:T(4,128)} %bitcast.5, s32[2,512]{1,0:T(2,128)} %couplings_hbm.1, f32[8]{0:T(128)} %k_hbm.1, f32[8]{0:T(128)} %lam_hbm.1), custom_call_target="tpu_custom_call" | custom-call | tf_op jit(solution)/shard_map/pallas_call | solution.py:655
  63.9 0.9 %add_bitcast_fusion = (f32[128,512]{1,0:T(8,128)}, f32[128,512]{1,0:T(8,128)}) fusion(f32[2,128,512]{2,1,0:T(8,128)S(1)} %get-tuple-element.5, f32[2,128,512]{2,1,0:T(8,128)S(1)} %get-tuple-element.4), kind=kLoop, calls=%fused_computation | loop fusion | flops 131072 | bytes 1572864 | tf_op jit(solution)/shard_map/add | solution.py:691
